TPU v7x, 128 devices: a whole 4x4x4 slice. The times are simulated.
128 devices in a mesh: shard: 16 (over y, z), tensor: 8 (over x, core).
Axes of the slice: x: 4, y: 4, z: 4, core: 2. Of those that a mesh axis runs over, the one named last changes fastest.
Arguments:
- grads: bfloat16 [32, 896, 16640], P('shard', None, 'tensor'), may hold values from -1 to 1
- small_grads: bfloat16 [32, 2944], P('shard', 'tensor'), may hold values from -6 to 6
- counts: int32 [16], P('shard'), may hold values from 1 to 2
- step: int32 [1], replicated, may hold values from 1 to 1000
- master: float32 [896, 16640], P(('shard', 'tensor')), may hold values from -0.01953125 to 0.01953125
- moment_one: float32 [896, 16640], P(('shard', 'tensor')), may hold values from -7.6293945e-05 to 7.6293945e-05
- moment_two: float32 [896, 16640], P(('shard', 'tensor')), may hold values from 1e-12 to 1e-09
- average: float32 [896, 16640], P(('shard', 'tensor')), may hold values from -0.01953125 to 0.01953125
- small_master: float32 [8, 368], P('tensor', 'shard'), may hold values from -0.046875 to 0.046875
- small_one: float32 [8, 368], P('tensor', 'shard'), may hold values from -0.0078125 to 0.0078125
- small_two: float32 [8, 368], P('tensor', 'shard'), may hold values from 1e-09 to 1e-07
- small_average: float32 [8, 368], P('tensor', 'shard'), may hold values from -0.046875 to 0.046875
Outputs:
- new_master: float32 [896, 16640], P(('shard', 'tensor'))
- new_one: float32 [896, 16640], P(('shard', 'tensor'))
- new_two: float32 [896, 16640], P(('shard', 'tensor'))
- small_new: float32 [8, 368], P('tensor', 'shard')
- small_new_one: float32 [8, 368], P('tensor', 'shard')
- small_new_two: float32 [8, 368], P('tensor', 'shard')
- weights_out: bfloat16 [896, 16640], P(None, 'tensor')
- small_weights_out: bfloat16 [2944], P('tensor')
- average_out: float32 [896, 16640], P(None, 'tensor')
- small_average_out: float32 [2944], P('tensor')
All inputs are finite; a program needn't handle non-finite values.
Results may differ from a plain program's by a relative error of at most 0.001.
Values may be sent and summed in bfloat16 or wider, within the bound.
A program may use at most 256 MiB of HBM per device.

v0:
```python
import jax
import jax.numpy as jnp
from jax import lax
from jax.sharding import PartitionSpec as P

learn_rate = 0.002
beta_one = 0.9
beta_two = 0.999
adam_eps = 1e-08
weight_decay = 0.1
clip_norm = 1.0
decay_rate = 0.99


def adam_update(param, first, second, gradient, time, decay):
    first_new = beta_one * first + (1.0 - beta_one) * gradient
    second_new = beta_two * second + (1.0 - beta_two) * gradient * gradient
    bias_one = 1.0 - jnp.power(jnp.float32(beta_one), time)
    bias_two = 1.0 - jnp.power(jnp.float32(beta_two), time)
    ratio = first_new / bias_one / (jnp.sqrt(second_new / bias_two) + adam_eps)
    param_new = param - learn_rate * (ratio + decay * param)
    return (param_new, first_new, second_new)


def shards(
    grads,
    small_grads,
    counts,
    step,
    master,
    moment_one,
    moment_two,
    average,
    small_master,
    small_one,
    small_two,
    small_average,
):
    micro = grads.shape[0]
    valid = (jnp.arange(micro, dtype=jnp.int32) < counts[0]).astype(jnp.float32)
    big_term = valid[0] * grads[0].astype(jnp.float32)
    small_term = valid[0] * small_grads[0].astype(jnp.float32)
    big_term = big_term + valid[1] * grads[1].astype(jnp.float32)
    small_term = small_term + valid[1] * small_grads[1].astype(jnp.float32)
    big_rows, small_part = (
        lax.psum_scatter(big_term, "shard", scatter_dimension=0, tiled=True),
        lax.psum_scatter(small_term, "shard", scatter_dimension=0, tiled=True),
    )
    flat_sum = lax.all_to_all(big_rows, "tensor", split_axis=0, concat_axis=1, tiled=True)
    small_part = small_part.reshape(1, -1)
    local_squares = jnp.sum(big_rows * big_rows) + jnp.sum(small_part * small_part)
    squares = lax.psum(local_squares, ("shard", "tensor"))
    norm = jnp.sqrt(squares)
    factor = jnp.minimum(1.0, clip_norm / (norm + 1e-06))
    time = step[0].astype(jnp.float32)
    new_master, new_one, new_two = adam_update(
        master, moment_one, moment_two, flat_sum * factor, time, weight_decay
    )
    small_new, small_new_one, small_new_two = adam_update(
        small_master, small_one, small_two, small_part * factor, time, 0.0
    )
    new_average = decay_rate * average + (1.0 - decay_rate) * new_master
    small_new_average = decay_rate * small_average + (1.0 - decay_rate) * small_new
    weights_flat = new_master.astype(jnp.bfloat16)
    small_weights = small_new.astype(jnp.bfloat16)
    weight_parts = lax.all_to_all(weights_flat, "tensor", split_axis=1, concat_axis=0, tiled=True)
    weight_blocks, small_all = (
        lax.all_gather(weight_parts, "shard", axis=0, tiled=True),
        lax.all_gather(small_weights, "shard", axis=1, tiled=True),
    )
    average_parts = lax.all_to_all(new_average, "tensor", split_axis=1, concat_axis=0, tiled=True)
    average_blocks, small_average_all = (
        lax.all_gather(average_parts, "shard", axis=0, tiled=True),
        lax.all_gather(small_new_average, "shard", axis=1, tiled=True),
    )
    return (
        new_master,
        new_one,
        new_two,
        small_new,
        small_new_one,
        small_new_two,
        weight_blocks,
        small_all.reshape(-1),
        average_blocks,
        small_average_all.reshape(-1),
    )


def solution(mesh):
    placed = (
        P("shard", None, "tensor"),
        P("shard", "tensor"),
        P("shard"),
        P(),
        P(("shard", "tensor"), None),
        P(("shard", "tensor"), None),
        P(("shard", "tensor"), None),
        P(("shard", "tensor"), None),
        P("tensor", "shard"),
        P("tensor", "shard"),
        P("tensor", "shard"),
        P("tensor", "shard"),
    )
    return jax.shard_map(
        shards,
        mesh=mesh,
        in_specs=placed,
        out_specs=(
            P(("shard", "tensor"), None),
            P(("shard", "tensor"), None),
            P(("shard", "tensor"), None),
            P("tensor", "shard"),
            P("tensor", "shard"),
            P("tensor", "shard"),
            P(None, "tensor"),
            P("tensor"),
            P(None, "tensor"),
            P("tensor"),
        ),
        check_vma=False,
    )
```

profile of v0, /device:TPU:1, one launch (start us, length us, event | category | flops | bytes accessed | tf_op | source)
XLA Modules:
  0.0 416.9 jit_solution(6151699952216724307)
XLA Ops:
  7.9 0.6 fusion.6
  8.5 8.8 %add_bitcast_fusion = f32[896,2080]{0,1:T(8,128)} fusion(bf16[2,896,2080]{1,2,0:T(8,128)(2,1)} %param.12, f32[]{:T(128)} %bitcast.4, f32[]{:T(128)} %bitcast.3), kind=kLoop, calls=%fused_computation | loop fusion | flops 9318400 | bytes 14909448 | tf_op jit(solution)/shard_map/add | solution.py:43
  17.3 0.6 copy-done.5
  17.9 0.6 fusion.5
  19.1 134.4 %all-reduce.6.cloned.1.call-done = f32[896,2080]{0,1:T(8,128)} async-done(((f32[896,2080]{0,1:T(8,128)}), f32[896,2080]{0,1:T(8,128)}) %all-reduce.6.cloned.1.call-update) | async-done | bytes 7454736
  153.5 2.5 multiply_reduce_fusion
  156.4 0.9 all_to_all.38
  157.3 4.9 %all-to-all-start = ((f32[8,7,2080]{2,1,0:T(8,128)}), f32[8,7,2080]{2,1,0:T(8,128)S(1)}, u32[]{:S(2)}, u32[]{:S(2)}) async-start(f32[8,7,2080]{2,1,0:T(8,128)} %all_to_all.38), calls=%async_computation | async-start | bytes 1114112 | tf_op jit(solution)/shard_map/all_to_all | solution.py:49
  163.6 1.3 add_reduce_fusion
  164.9 30.9 %all-reduce.3 = f32[368]{0:T(512)S(1)} all-reduce(f32[368]{0:T(512)S(1)} %add_reduce_fusion), channel_id=3, replica_groups=mesh['shard'=16,'tensor'=8] {'shard'}, use_global_device_ids=true, to_apply=%region_2.0.clone | all-reduce | flops 368 | bytes 2944
  195.8 0.7 multiply_reduce_fusion.1
  197.8 69.7 %psum.7 = f32[]{:T(128)} all-reduce(f32[]{:T(128)S(6)} %add.61), channel_id=1, replica_groups=mesh['shard'=16,'tensor'=8] {'shard','tensor'}, use_global_device_ids=true, to_apply=%region_4.0 | all-reduce | flops 1 | bytes 8 | tf_op jit(solution)/shard_map/psum | solution.py:52
  268.7 2.5 multiply_add_fusion
  271.2 0.5 all_to_all.40
  271.7 11.8 %all_to_all.51 = bf16[7,8,2080]{2,0,1:T(8,128)(2,1)S(1)} all-to-all(bf16[7,8,2080]{2,0,1:T(8,128)(2,1)S(1)} %copy.38), channel_id=1, replica_groups=mesh['shard'=16,'tensor'=8] {'tensor'}, dimensions={1} | all-to-all | bytes 465920 | tf_op jit(solution)/shard_map/all_to_all | solution.py:66
  283.6 0.8 all_to_all.43
  285.0 13.0 %all_to_all.52 = f32[7,8,2080]{2,0,1:T(8,128)S(1)} all-to-all(f32[7,8,2080]{2,0,1:T(8,128)S(1)} %copy.39), channel_id=1, replica_groups=mesh['shard'=16,'tensor'=8] {'tensor'}, dimensions={1} | all-to-all | bytes 931840 | tf_op jit(solution)/shard_map/all_to_all | solution.py:71
  298.1 0.8 all_to_all.47
  299.6 0.6 bitcast_dynamic-update-slice_fusion
  300.5 30.7 %all-reduce = bf16[368]{0:T(512)(128)(2,1)} all-reduce(bf16[368]{0:T(512)(128)(2,1)S(1)} %dynamic-update-slice), channel_id=1, replica_groups=mesh['shard'=16,'tensor'=8] {'shard'}, use_global_device_ids=true, to_apply=%add | all-reduce | flops 368 | bytes 1472 | tf_op jit(solution)/shard_map/reshape | solution.py:84
  331.2 30.5 %all-reduce.1 = f32[368]{0:T(512)} all-reduce(f32[368]{0:T(512)S(1)} %get-tuple-element.40), channel_id=1, replica_groups=mesh['shard'=16,'tensor'=8] {'shard'}, use_global_device_ids=true, to_apply=%add.1 | all-reduce | flops 368 | bytes 2944 | tf_op jit(solution)/shard_map/reshape | solution.py:86
  361.7 6.1 %copy.40 = bf16[896,2080]{0,1:T(8,128)(2,1)} copy(bf16[896,2080]{1,0:T(8,128)(2,1)} %all-gather.3.cloned.1.call-done) | data formatting | bytes 7454720
  367.8 34.0 %all-gather.5.cloned.1.call-done = f32[896,2080]{1,0:T(8,128)} async-done(((f32[56,2080]{1,0:T(8,128)}), f32[896,2080]{1,0:T(8,128)}) %all-gather.5.cloned.1.call-update) | async-done | bytes 7454736 | tf_op jit(solution)/shard_map/all_gather | solution.py:73
  401.8 8.6 %copy.41 = f32[896,2080]{0,1:T(8,128)} copy(f32[896,2080]{1,0:T(8,128)} %all-gather.5.cloned.1.call-done) | data formatting | bytes 14909440
  (42 shorter events, 1.8 us)
Async XLA Ops:
  7.2 146.3 %all-reduce.6.cloned.1.call-start = ((), (), s32[]{:S(2)}) async-start(), calls=%async_computation.5 | async-start | bytes 14909440
  17.2 0.7 copy-start.5
  17.2 146.3 %copy-start.4 = (bf16[2,368]{1,0:T(2,128)(2,1)S(1)}, bf16[2,368]{1,0:T(2,128)(2,1)}, u32[]{:S(2)}) copy-start(bf16[2,368]{1,0:T(2,128)(2,1)} %param.13) | copy-start | bytes 4420
  17.2 251.5 %copy-start.1 = (f32[7,16640]{1,0:T(8,128)S(1)}, f32[7,16640]{1,0:T(8,128)}, u32[]{:S(2)}) copy-start(f32[7,16640]{1,0:T(8,128)} %param.19) | copy-start | bytes 1397764
  17.2 251.5 %copy-start.2 = (f32[7,16640]{1,0:T(8,128)S(1)}, f32[7,16640]{1,0:T(8,128)}, u32[]{:S(2)}) copy-start(f32[7,16640]{1,0:T(8,128)} %param.16) | copy-start | bytes 1397764
  17.2 251.5 %copy-start.3 = (f32[7,16640]{1,0:T(8,128)S(1)}, f32[7,16640]{1,0:T(8,128)}, u32[]{:S(2)}) copy-start(f32[7,16640]{1,0:T(8,128)} %param.18) | copy-start | bytes 1397764
  157.3 111.0 %all-to-all-start = ((f32[8,7,2080]{2,1,0:T(8,128)}), f32[8,7,2080]{2,1,0:T(8,128)S(1)}, u32[]{:S(2)}, u32[]{:S(2)}) async-start(f32[8,7,2080]{2,1,0:T(8,128)} %all_to_all.38), calls=%async_computation | async-start | bytes 1114112 | tf_op jit(solution)/shard_map/all_to_all | solution.py:49
  162.2 199.5 %all-gather.3.cloned.1.call-start = ((), (), s32[]{:S(2)}) async-start(), calls=%async_computation.3 | async-start | bytes 4143104 | tf_op jit(solution)/shard_map/all_gather | solution.py:68
  268.3 31.3 %copy-start.6 = (f32[1,23]{1,0:T(1,128)S(1)}, f32[1,23]{1,0:T(1,128)}, u32[]{:S(2)}) copy-start(f32[1,23]{1,0:T(1,128)} %param.23) | copy-start | bytes 280
  268.3 31.3 %copy-start.7 = (f32[1,23]{1,0:T(1,128)S(1)}, f32[1,23]{1,0:T(1,128)}, u32[]{:S(2)}) copy-start(f32[1,23]{1,0:T(1,128)} %param.20) | copy-start | bytes 280
  268.3 31.3 %copy-start.8 = (f32[1,23]{1,0:T(1,128)S(1)}, f32[1,23]{1,0:T(1,128)}, u32[]{:S(2)}) copy-start(f32[1,23]{1,0:T(1,128)} %param.22) | copy-start | bytes 280
  268.3 31.3 %copy-start.9 = (f32[1,23]{1,0:T(1,128)S(1)}, f32[1,23]{1,0:T(1,128)}, u32[]{:S(2)}) copy-start(f32[1,23]{1,0:T(1,128)} %param.21) | copy-start | bytes 280
  271.2 96.6 %copy-start = (f32[7,16640]{1,0:T(8,128)}, f32[7,16640]{1,0:T(8,128)S(1)}, u32[]{:S(2)}) copy-start(f32[7,16640]{1,0:T(8,128)S(1)} %get-tuple-element.45) | copy-start | bytes 1397764
  284.4 117.4 %all-gather.5.cloned.1.call-start = ((), (), s32[]{:S(2)}) async-start(), calls=%async_computation.4 | async-start | bytes 8286208 | tf_op jit(solution)/shard_map/all_gather | solution.py:73
  300.2 110.1 %copy-start.10 = (f32[1,23]{1,0:T(1,128)}, f32[1,23]{1,0:T(1,128)S(1)}, u32[]{:S(2)}) copy-start(f32[1,23]{1,0:T(1,128)S(1)} %get-tuple-element.41) | copy-start | bytes 280
Sparse Core Ops, SparseCore 0:
  17.4 136.0 all-reduce.5
  284.6 46.2 all-gather.2
  333.9 67.8 all-gather.4
where the time goes:
time: 418 us; the launch traced here: 417 us
  blocking collectives  187 us (45%)
  waiting for transfers between devices  168 us (40%)
  local copies, waits for them, and re-layouts  21.1 us (5%)
  between operations  19.3 us (5%)
  other arithmetic  16.5 us (4%)
  starting transfers between devices  5.01 us (1%)
    unnamed x4, waiting for transfers between devices  134 us
    psum x1, blocking collectives, shards(): squares = lax.psum(local_squares, ('shard', 'tensor'))  69.7 us
    all_gather x1, waiting for transfers between devices, shards(): lax.all_gather(average_parts, 'shard', axis=0, tiled=True)  34 us
    unnamed x1, blocking collectives  30.9 us
    reshape x1, blocking collectives, shards(): small_all.reshape(-1)  30.7 us
    reshape x1, blocking collectives, shards(): small_average_all.reshape(-1)  30.5 us
    unnamed x28, local copies, waits for them, and re-layouts  16.2 us
    all_to_all x1, blocking collectives, shards(): lax.all_to_all(new_average, 'tensor', split_axis=1, concat_axis=0, tiled=...  13 us
  transfers between devices with their start and end apart: 4, of which 2 were waited for; matrix products, arithmetic and copies ran while one was open for 2% of the time, Pallas kernels for 0%

commit v1 on v0

--- a/solution.py
+++ b/solution.py
@@ -70,7 +70,10 @@
     )
     average_parts = lax.all_to_all(new_average, "tensor", split_axis=1, concat_axis=0, tiled=True)
     average_blocks, small_average_all = (
-        lax.all_gather(average_parts, "shard", axis=0, tiled=True),
+        jnp.concatenate(
+            lax.all_to_all(jnp.stack([average_parts] * lax.axis_size("shard")), "shard", 0, 0),
+            axis=0,
+        ),
         lax.all_gather(small_new_average, "shard", axis=1, tiled=True),
     )
     return (

time: 418 us -> 534 us (1.28)
  the two profiles are of different devices: /device:TPU:1 before, /device:TPU:34 now
where the time goes in v1:
time: 534 us; the launch traced here: 533 us
  blocking collectives  304 us (57%)
  waiting for transfers between devices  146 us (27%)
  local copies, waits for them, and re-layouts  25.4 us (5%)
  starting transfers between devices  20.9 us (4%)
  between operations  19.6 us (4%)
  other arithmetic  16.5 us (3%)
    reshape x1, blocking collectives, shards(): small_all.reshape(-1)  163 us
    unnamed x3, waiting for transfers between devices  133 us
    psum x1, blocking collectives, shards(): squares = lax.psum(local_squares, ('shard', 'tensor'))  63.4 us
    reshape x1, blocking collectives, shards(): small_average_all.reshape(-1)  41.6 us
    unnamed x1, blocking collectives  36.3 us
    unnamed x28, local copies, waits for them, and re-layouts  16.2 us
  transfers between devices with their start and end apart: 6, of which 3 were waited for; matrix products, arithmetic and copies ran while one was open for 3% of the time, Pallas kernels for 0%

profile of v1, /device:TPU:34, one launch (start us, length us, event | category | flops | bytes accessed | tf_op | source)
XLA Modules:
  0.0 533.0 jit_solution(2798444342806077109)
XLA Ops:
  8.5 8.8 %add_bitcast_fusion = f32[896,2080]{0,1:T(8,128)} fusion(bf16[2,896,2080]{1,2,0:T(8,128)(2,1)} %param.12, f32[]{:T(128)} %bitcast.4, f32[]{:T(128)} %bitcast.3), kind=kLoop, calls=%fused_computation | loop fusion | flops 9318400 | bytes 14909448 | tf_op jit(solution)/shard_map/add | solution.py:43
  19.1 132.7 %all-reduce.6.cloned.1.call-done = f32[896,2080]{0,1:T(8,128)} async-done(((f32[896,2080]{0,1:T(8,128)}), f32[896,2080]{0,1:T(8,128)}) %all-reduce.6.cloned.1.call-update) | async-done | bytes 7454736
  151.9 2.5 multiply_reduce_fusion
  154.7 0.9 all_to_all.39
  155.6 4.8 all-to-all-start
  161.8 1.3 add_reduce_fusion
  163.1 36.3 %all-reduce.3 = f32[368]{0:T(512)S(1)} all-reduce(f32[368]{0:T(512)S(1)} %add_reduce_fusion), channel_id=3, replica_groups=mesh['shard'=16,'tensor'=8] {'shard'}, use_global_device_ids=true, to_apply=%region_2.0.clone | all-reduce | flops 368 | bytes 2944
  199.5 0.7 multiply_reduce_fusion.1
  201.5 63.4 %psum.7 = f32[]{:T(128)} all-reduce(f32[]{:T(128)S(6)} %add.61), channel_id=1, replica_groups=mesh['shard'=16,'tensor'=8] {'shard','tensor'}, use_global_device_ids=true, to_apply=%region_4.0 | all-reduce | flops 1 | bytes 8 | tf_op jit(solution)/shard_map/psum | solution.py:52
  266.0 2.5 multiply_add_fusion
  269.0 0.7 copy.37
  269.8 5.1 all-to-all-start.1
  275.3 0.9 copy.38
  276.2 5.0 all-to-all-done.1
  281.2 4.9 all-to-all-start.2
  286.1 0.8 all_to_all.44
  286.9 8.4 %all-to-all-done.2 = f32[7,8,2080]{2,0,1:T(8,128)S(1)} async-done(((f32[7,8,2080]{2,0,1:T(8,128)}), f32[7,8,2080]{2,0,1:T(8,128)S(1)}, u32[]{:S(2)}, u32[]{:S(2)}) %all-to-all-start.2) | async-done | bytes 465952 | tf_op jit(solution)/shard_map/all_to_all | solution.py:71
  295.4 3.6 stack.5
  299.1 6.0 %all-to-all-start.3 = ((f32[16,56,2080]{2,1,0:T(8,128)}), f32[16,56,2080]{2,1,0:T(8,128)}, u32[]{:S(2)}, u32[]{:S(2)}) async-start(f32[16,56,2080]{2,1,0:T(8,128)} %stack.5), calls=%async_computation.3 | async-start | bytes 15597568 | tf_op jit(solution)/shard_map/all_to_all | solution.py:74
  305.8 0.6 bitcast_dynamic-update-slice_fusion
  306.7 163.1 %all-reduce = bf16[368]{0:T(512)(128)(2,1)} all-reduce(bf16[368]{0:T(512)(128)(2,1)S(1)} %dynamic-update-slice), channel_id=1, replica_groups=mesh['shard'=16,'tensor'=8] {'shard'}, use_global_device_ids=true, to_apply=%add | all-reduce | flops 368 | bytes 1472 | tf_op jit(solution)/shard_map/reshape | solution.py:87
  469.8 41.6 %all-reduce.1 = f32[368]{0:T(512)} all-reduce(f32[368]{0:T(512)S(1)} %get-tuple-element.40), channel_id=1, replica_groups=mesh['shard'=16,'tensor'=8] {'shard'}, use_global_device_ids=true, to_apply=%add.1 | all-reduce | flops 368 | bytes 2944 | tf_op jit(solution)/shard_map/reshape | solution.py:89
  511.4 6.1 %copy.39 = bf16[896,2080]{0,1:T(8,128)(2,1)} copy(bf16[896,2080]{1,0:T(8,128)(2,1)} %all-gather.2.cloned.1.call-done) | data formatting | bytes 7454720
  517.5 8.6 %copy.40 = f32[896,2080]{0,1:T(8,128)} copy(f32[896,2080]{1,0:T(8,128)} %bitcast.16) | data formatting | bytes 14909440
  (44 shorter events, 3.9 us)
Async XLA Ops:
  7.2 144.7 %all-reduce.6.cloned.1.call-start = ((), (), s32[]{:S(2)}) async-start(), calls=%async_computation.5 | async-start | bytes 14909440
  17.2 0.7 copy-start.5
  17.2 144.6 %copy-start.4 = (bf16[2,368]{1,0:T(2,128)(2,1)S(1)}, bf16[2,368]{1,0:T(2,128)(2,1)}, u32[]{:S(2)}) copy-start(bf16[2,368]{1,0:T(2,128)(2,1)} %param.13) | copy-start | bytes 4420
  17.2 248.8 %copy-start.1 = (f32[7,16640]{1,0:T(8,128)S(1)}, f32[7,16640]{1,0:T(8,128)}, u32[]{:S(2)}) copy-start(f32[7,16640]{1,0:T(8,128)} %param.19) | copy-start | bytes 1397764
  17.2 248.8 %copy-start.2 = (f32[7,16640]{1,0:T(8,128)S(1)}, f32[7,16640]{1,0:T(8,128)}, u32[]{:S(2)}) copy-start(f32[7,16640]{1,0:T(8,128)} %param.16) | copy-start | bytes 1397764
  17.2 248.8 %copy-start.3 = (f32[7,16640]{1,0:T(8,128)S(1)}, f32[7,16640]{1,0:T(8,128)}, u32[]{:S(2)}) copy-start(f32[7,16640]{1,0:T(8,128)} %param.18) | copy-start | bytes 1397764
  155.6 110.0 %all-to-all-start = ((f32[8,7,2080]{2,1,0:T(8,128)}), f32[8,7,2080]{2,1,0:T(8,128)S(1)}, u32[]{:S(2)}, u32[]{:S(2)}) async-start(f32[8,7,2080]{2,1,0:T(8,128)} %all_to_all.39), calls=%async_computation | async-start | bytes 1114112 | tf_op jit(solution)/shard_map/all_to_all | solution.py:49
  268.5 30.5 %copy-start = (f32[7,16640]{1,0:T(8,128)}, f32[7,16640]{1,0:T(8,128)S(1)}, u32[]{:S(2)}) copy-start(f32[7,16640]{1,0:T(8,128)S(1)} %get-tuple-element.45) | copy-start | bytes 1397764
  269.8 11.4 %all-to-all-start.1 = ((bf16[7,8,2080]{2,0,1:T(8,128)(2,1)}), bf16[7,8,2080]{2,0,1:T(8,128)(2,1)S(1)}, u32[]{:S(2)}, u32[]{:S(2)}) async-start(bf16[7,8,2080]{2,0,1:T(8,128)(2,1)} %copy.37), calls=%async_computation.1 | async-start | bytes 557056 | tf_op jit(solution)/shard_map/all_to_all | solution.py:66
  281.2 14.2 %all-to-all-start.2 = ((f32[7,8,2080]{2,0,1:T(8,128)}), f32[7,8,2080]{2,0,1:T(8,128)S(1)}, u32[]{:S(2)}, u32[]{:S(2)}) async-start(f32[7,8,2080]{2,0,1:T(8,128)} %copy.38), calls=%async_computation.2 | async-start | bytes 1114112 | tf_op jit(solution)/shard_map/all_to_all | solution.py:71
  286.1 225.3 %all-gather.2.cloned.1.call-start = ((), (), s32[]{:S(2)}) async-start(), calls=%async_computation.4 | async-start | bytes 4143104 | tf_op jit(solution)/shard_map/all_gather | solution.py:68
  299.0 6.7 %copy-start.6 = (f32[1,23]{1,0:T(1,128)S(1)}, f32[1,23]{1,0:T(1,128)}, u32[]{:S(2)}) copy-start(f32[1,23]{1,0:T(1,128)} %param.23) | copy-start | bytes 280
  299.0 6.7 %copy-start.7 = (f32[1,23]{1,0:T(1,128)S(1)}, f32[1,23]{1,0:T(1,128)}, u32[]{:S(2)}) copy-start(f32[1,23]{1,0:T(1,128)} %param.20) | copy-start | bytes 280
  299.0 6.7 %copy-start.8 = (f32[1,23]{1,0:T(1,128)S(1)}, f32[1,23]{1,0:T(1,128)}, u32[]{:S(2)}) copy-start(f32[1,23]{1,0:T(1,128)} %param.22) | copy-start | bytes 280
  299.1 6.7 %copy-start.9 = (f32[1,23]{1,0:T(1,128)S(1)}, f32[1,23]{1,0:T(1,128)}, u32[]{:S(2)}) copy-start(f32[1,23]{1,0:T(1,128)} %param.21) | copy-start | bytes 280
  299.1 218.5 %all-to-all-start.3 = ((f32[16,56,2080]{2,1,0:T(8,128)}), f32[16,56,2080]{2,1,0:T(8,128)}, u32[]{:S(2)}, u32[]{:S(2)}) async-start(f32[16,56,2080]{2,1,0:T(8,128)} %stack.5), calls=%async_computation.3 | async-start | bytes 15597568 | tf_op jit(solution)/shard_map/all_to_all | solution.py:74
  306.4 219.7 %copy-start.10 = (f32[1,23]{1,0:T(1,128)}, f32[1,23]{1,0:T(1,128)S(1)}, u32[]{:S(2)}) copy-start(f32[1,23]{1,0:T(1,128)S(1)} %get-tuple-element.41) | copy-start | bytes 280
Sparse Core Ops, SparseCore 0:
  17.4 134.4 all-reduce.5
  289.9 137.5 all-gather.1
